TPU v7x, 256 devices: a whole 4x4x8 slice. The times are simulated.
256 devices in a mesh: node: 64 (over y, z, core), feat: 4 (over x).
Axes of the slice: x: 4, y: 4, z: 8, core: 2. Of those that a mesh axis runs over, the one named last changes fastest.
Arguments:
- features: bfloat16 [32768, 128], P('node', 'feat'), may hold values from -10 to 10
- send_rows: int32 [64, 64, 64], P('node'), may hold values from 0 to 511
- send_count: int32 [64, 64], P('node'), may hold values from 1 to 64, 2048 in all within a row
- tile_src: int32 [256, 16], P('node'), may hold values from 0 to 35
- tile_val: bfloat16 [256, 16, 128, 128], P('node'), may hold values from 0 to 0.0009765625
- labels: int32 [32768], P('node'), may hold values from 0 to 171
- w_self1: bfloat16 [128, 1024], P('feat'), may hold values from -0.5 to 0.5
- w_neigh1: bfloat16 [128, 1024], P('feat'), may hold values from -0.5 to 0.5
- w_self2: bfloat16 [1024, 172], P('feat'), may hold values from -0.5 to 0.5
- w_neigh2: bfloat16 [1024, 172], P('feat'), may hold values from -0.1875 to 0.1875
Outputs:
- mean_loss: float32 [], replicated
- grad_self1: float32 [128, 1024], P('feat')
- grad_neigh1: float32 [128, 1024], P('feat')
- grad_self2: float32 [1024, 172], P('feat')
- grad_neigh2: float32 [1024, 172], P('feat')
Inputs may be any that keep to these rules, and one draw needn't show every extreme that they name: `send_rows`: row indices within the sending partition's 512 rows. Each row of send_count sums to 2048 and holds 64 at least once. `tile_src`: block numbers of the destination partition's source rows: numbers below 4 name its own rows, the others its halo slots.
All inputs are finite; a program needn't handle non-finite values.
Results may differ from a plain program's by a relative error of at most 0.00095.
The roundings to bfloat16 on the way count: a program that leaves them out, or rounds other values in their place, can miss the bound.
Values may be sent and summed in bfloat16 or wider, within the bound.
A program may use at most 64 MiB of HBM per device.

v0:
```python
import math
import jax
import jax.numpy as jnp
from jax import lax
from jax.sharding import PartitionSpec as P


def pack_rows(own_rows, send_rows, send_count):
    slot_total = send_rows.shape[2]
    picked = jnp.take(own_rows, send_rows[0].reshape(-1), axis=0)
    picked = picked.reshape(send_rows.shape[1], slot_total, own_rows.shape[1])
    in_use = jnp.arange(slot_total, dtype=jnp.int32)[None, :] < send_count[0][:, None]
    return jnp.where(in_use[:, :, None], picked, jnp.zeros_like(picked))


def aggregate(own_rows, arrived, tile_src, tile_val):
    col_count = own_rows.shape[1]
    blocks = jnp.concatenate([own_rows, arrived], axis=0).reshape(-1, 128, col_count)
    chosen = jnp.take(blocks, tile_src, axis=0)
    summed = jnp.einsum("bkij,bkjh->bih", tile_val, chosen, preferred_element_type=jnp.float32)
    return summed.reshape(own_rows.shape[0], col_count).astype(jnp.bfloat16)


def spread_back(grads, tile_src, tile_val, src_total):
    col_count = grads.shape[1]
    per_tile = jnp.einsum(
        "bkij,bih->bkjh",
        tile_val,
        grads.reshape(-1, 128, col_count),
        preferred_element_type=jnp.float32,
    )
    one_hot = (
        tile_src.reshape(-1)[None, :] == jnp.arange(src_total // 128, dtype=jnp.int32)[:, None]
    ).astype(jnp.float32)
    landed = jnp.dot(
        one_hot,
        per_tile.reshape(one_hot.shape[1], -1),
        precision=lax.Precision.HIGHEST,
        preferred_element_type=jnp.float32,
    )
    return landed.reshape(src_total, col_count)


def cross_entropy(logits, labels, grad_scale):
    row_max = jnp.max(logits, axis=1, keepdims=True)
    shifted = logits - row_max
    total_exp = jnp.sum(jnp.exp(shifted), axis=1, keepdims=True)
    classes = jnp.arange(logits.shape[1], dtype=jnp.int32)
    target = (labels[:, None] == classes[None, :]).astype(jnp.float32)
    row_loss = jnp.log(total_exp)[:, 0] - jnp.sum(shifted * target, axis=1)
    grads = ((jnp.exp(shifted) / total_exp - target) * grad_scale).astype(jnp.bfloat16)
    return (row_loss, grads)


def shards(
    features,
    send_rows,
    send_count,
    tile_src,
    tile_val,
    labels,
    w_self1,
    w_neigh1,
    w_self2,
    w_neigh2,
):
    node_count = lax.axis_size("node")
    own_count = features.shape[0]
    slot_total = send_rows.shape[2]
    src_total = own_count + node_count * slot_total
    node_total = own_count * node_count
    grad_scale = 1.0 / math.sqrt(node_total)
    outgoing = pack_rows(features, send_rows, send_count)
    arrived = lax.all_to_all(outgoing, "node", split_axis=0, concat_axis=0, tiled=True).reshape(
        -1, features.shape[1]
    )
    agg_one = aggregate(features, arrived, tile_src, tile_val)
    partial_one = jnp.dot(features, w_self1, preferred_element_type=jnp.float32)
    partial_one = partial_one + jnp.dot(agg_one, w_neigh1, preferred_element_type=jnp.float32)
    pre_act = lax.psum_scatter(partial_one, "feat", scatter_dimension=1, tiled=True)
    activated, pullback = jax.vjp(lambda inner: jax.nn.gelu(inner, approximate=True), pre_act)
    hidden = activated.astype(jnp.bfloat16)
    unit_count = hidden.shape[1]
    outgoing_two = pack_rows(hidden, send_rows, send_count)
    arrived_two = lax.all_to_all(
        outgoing_two, "node", split_axis=0, concat_axis=0, tiled=True
    ).reshape(-1, unit_count)
    agg_two = aggregate(hidden, arrived_two, tile_src, tile_val)
    partial_two = jnp.dot(hidden, w_self2, preferred_element_type=jnp.float32)
    partial_two = partial_two + jnp.dot(agg_two, w_neigh2, preferred_element_type=jnp.float32)
    logits = lax.psum(partial_two, "feat")
    row_loss, dlogits = cross_entropy(logits, labels, grad_scale)
    mean_loss = lax.psum(jnp.sum(row_loss), "node") / node_total
    grad_pair = lax.psum(
        (
            jnp.einsum("nh,nc->hc", hidden, dlogits, preferred_element_type=jnp.float32),
            jnp.einsum("nh,nc->hc", agg_two, dlogits, preferred_element_type=jnp.float32),
        ),
        "node",
    )
    back_grad = jnp.einsum(
        "nc,hc->nh", dlogits, w_neigh2, preferred_element_type=jnp.float32
    ).astype(jnp.bfloat16)
    direct = jnp.einsum("nc,hc->nh", dlogits, w_self2, preferred_element_type=jnp.float32)
    landed = spread_back(back_grad, tile_src, tile_val, src_total)
    halo_back = landed[own_count:].reshape(node_count, slot_total, unit_count)
    returned = lax.all_to_all(
        halo_back.astype(jnp.bfloat16), "node", split_axis=0, concat_axis=0, tiled=True
    ).astype(halo_back.dtype)
    in_use = jnp.arange(slot_total, dtype=jnp.int32)[None, :] < send_count[0][:, None]
    returned = jnp.where(in_use[:, :, None], returned, jnp.zeros_like(returned))
    back_rows = jax.ops.segment_sum(
        returned.reshape(-1, unit_count), send_rows[0].reshape(-1), num_segments=own_count
    )
    back_hidden = direct + landed[:own_count] + back_rows
    pre_grad = pullback(back_hidden)[0].astype(jnp.bfloat16)
    shard_piece = lax.all_gather(pre_grad, "feat", axis=1, tiled=True)
    local_grads = jnp.stack(
        [
            jnp.einsum("nf,nh->fh", features, shard_piece, preferred_element_type=jnp.float32),
            jnp.einsum("nf,nh->fh", agg_one, shard_piece, preferred_element_type=jnp.float32),
        ]
    )
    summed = lax.psum(local_grads, "node")
    return (mean_loss, summed[0], summed[1], grad_pair[0], grad_pair[1])


def solution(mesh):
    in_specs = (
        P("node", "feat"),
        P("node", None, None),
        P("node", None),
        P("node", None),
        P("node", None, None, None),
        P("node"),
        P("feat", None),
        P("feat", None),
        P("feat", None),
        P("feat", None),
    )
    out_specs = (P(), P("feat", None), P("feat", None), P("feat", None), P("feat", None))
    return jax.shard_map(shards, mesh=mesh, in_specs=in_specs, out_specs=out_specs, check_vma=False)
```

profile of v0, /device:TPU:2, one launch (start us, length us, event | category | flops | bytes accessed | tf_op | source)
XLA Modules:
  0.0 571.0 jit_solution(3139560621322994043)
XLA Ops:
  10.0 12.1 %gather_fusion = bf16[4096,32]{1,0:T(8,128)(2,1)S(1)} fusion(bf16[512,32]{1,0:T(8,128)(2,1)S(1)} %copy.35, s32[4096]{0:T(1024)S(1)} %broadcast_clamp_fusion), kind=kCustom, calls=%fused_computation | custom fusion | bytes 540672 | tf_op jit(solution)/shard_map/jit(_take)/gather | solution.py:10
  25.4 12.1 %all-to-all-start = ((bf16[64,2,1024]{2,1,0:T(2,128)(2,1)}), bf16[64,2,1024]{2,1,0:T(2,128)(2,1)S(1)}, u32[]{:S(2)}, u32[]{:S(2)}) async-start(bf16[64,2,1024]{2,1,0:T(2,128)(2,1)} %reshape.178), calls=%async_computation | async-start | bytes 524288 | tf_op jit(solution)/shard_map/all_to_all | solution.py:74
  37.7 1.8 fusion.31
  39.5 10.0 %all-to-all-done = bf16[64,2,1024]{2,1,0:T(2,128)(2,1)S(1)} async-done(((bf16[64,2,1024]{2,1,0:T(2,128)(2,1)}), bf16[64,2,1024]{2,1,0:T(2,128)(2,1)S(1)}, u32[]{:S(2)}, u32[]{:S(2)}) %all-to-all-start) | async-done | bytes 262176 | tf_op jit(solution)/shard_map/all_to_all | solution.py:74
  52.9 1.8 convolution_add_fusion
  54.7 28.0 %reduce-scatter.2.cloned.1.call-done = f32[512,256]{1,0:T(8,128)} async-done(((f32[512,1024]{1,0:T(8,128)}), f32[512,256]{1,0:T(8,128)}) %reduce-scatter.2.cloned.1.call-update) | async-done | bytes 524304 | tf_op jit(solution)/shard_map/reduce_scatter | solution.py:80
  83.9 16.9 %gather_fusion.2 = bf16[4096,256]{1,0:T(8,128)(2,1)} fusion(bf16[512,256]{1,0:T(8,128)(2,1)S(1)} %multiply_convert_fusion, s32[4096]{0:T(1024)S(1)} %broadcast_clamp_fusion), kind=kCustom, calls=%fused_computation.2 | custom fusion | bytes 4210688 | tf_op jit(solution)/shard_map/jit(_take)/gather | solution.py:10
  100.8 4.4 select_select_fusion
  105.2 10.9 %all-to-all-start.1 = ((bf16[64,64,256]{2,1,0:T(8,128)(2,1)}), bf16[64,64,256]{2,1,0:T(8,128)(2,1)}, u32[]{:S(2)}, u32[]{:S(2)}) async-start(bf16[64,64,256]{2,1,0:T(8,128)(2,1)} %select_select_fusion), calls=%async_computation.2 | async-start | bytes 4194304 | tf_op jit(solution)/shard_map/all_to_all | solution.py:85
  116.4 50.7 %all-to-all-done.1 = bf16[64,64,256]{2,1,0:T(8,128)(2,1)} async-done(((bf16[64,64,256]{2,1,0:T(8,128)(2,1)}), bf16[64,64,256]{2,1,0:T(8,128)(2,1)}, u32[]{:S(2)}, u32[]{:S(2)}) %all-to-all-start.1) | async-done | bytes 2097184 | tf_op jit(solution)/shard_map/all_to_all | solution.py:85
  167.1 3.2 pad_maximum_fusion
  170.3 4.4 gather_fusion.3
  174.7 3.2 fusion.7
  179.0 42.6 %all-reduce.4.cloned.1.call-done = f32[512,172]{0,1:T(8,128)} async-done(((f32[512,172]{0,1:T(8,128)}), f32[512,172]{0,1:T(8,128)}) %all-reduce.4.cloned.1.call-update) | async-done | bytes 352272 | tf_op jit(solution)/shard_map/psum | solution.py:91
  225.2 4.5 convolution_bitcast_fusion
  229.7 8.7 %copy.41 = f32[4,16,128,256]{3,2,1,0:T(8,128)} copy(f32[4,16,128,256]{2,3,1,0:T(8,128)} %convolution_bitcast_fusion) | data formatting | bytes 16777216 | tf_op jit(solution)/shard_map/bkij,bih->bkjh/dot_general | solution.py:26
  238.4 8.1 %copy.49 = f32[8,8,128,256]{3,1,2,0:T(8,128)S(1)} copy(f32[8,8,128,256]{3,2,1,0:T(8,128)} %bitcast.90) | data formatting | bytes 16777216
  246.5 4.3 fusion.26
  250.8 2.3 copy-done.2
  253.4 2.4 convert_element_type.51
  255.9 10.9 %all-to-all-start.2 = ((bf16[64,64,256]{2,1,0:T(8,128)(2,1)}), bf16[64,64,256]{2,1,0:T(8,128)(2,1)}, u32[]{:S(2)}, u32[]{:S(2)}) async-start(bf16[64,64,256]{2,1,0:T(8,128)(2,1)} %convert_element_type.51), calls=%async_computation.3 | async-start | bytes 4194304 | tf_op jit(solution)/shard_map/all_to_all | solution.py:107
  267.5 50.3 %all-to-all-done.2 = bf16[64,64,256]{2,1,0:T(8,128)(2,1)} async-done(((bf16[64,64,256]{2,1,0:T(8,128)(2,1)}), bf16[64,64,256]{2,1,0:T(8,128)(2,1)}, u32[]{:S(2)}, u32[]{:S(2)}) %all-to-all-start.2) | async-done | bytes 2097184 | tf_op jit(solution)/shard_map/all_to_all | solution.py:107
  317.8 3.5 convert_select_fusion
  321.3 23.3 %scatter_fusion = f32[512,256]{1,0:T(8,128)S(1)} fusion(f32[512,256]{1,0:T(8,128)S(1)} %convolution_add_fusion.1, s32[4096]{0:T(1024)S(1)} %reshape.164, f32[4096,256]{1,0:T(8,128)} %bitcast.92), kind=kCustom, calls=%fused_computation.4 | custom fusion | flops 1048576 | bytes 12599296 | tf_op jit(solution)/shard_map/scatter-add | solution.py:112
  347.5 23.0 %all-gather.2.cloned.1.call-done = bf16[512,1024]{1,0:T(8,128)(2,1)} async-done(((bf16[512,256]{1,0:T(8,128)(2,1)}), bf16[512,1024]{1,0:T(8,128)(2,1)}) %all-gather.2.cloned.1.call-update) | async-done | bytes 1048592 | tf_op jit(solution)/shard_map/all_gather | solution.py:117
  370.5 1.7 convolution_bitcast_fusion.2
  372.2 1.5 convolution_bitcast_fusion.1
  375.0 128.7 %psum.36 = f32[]{:T(128)} all-reduce(f32[]{:T(128)} %subtract_reduce_fusion), channel_id=1, replica_groups=mesh['node'=64,'feat'=4] {'node'}, use_global_device_ids=true, to_apply=%region_6.7 | all-reduce | flops 1 | bytes 8 | tf_op jit(solution)/shard_map/psum | solution.py:93
  504.4 54.0 %all-reduce.6.cloned.1.call-done = (f32[2,32,1024]{2,1,0:T(8,128)}, f32[256,172]{0,1:T(8,128)}, f32[256,172]{0,1:T(8,128)}) async-done(((f32[2,32,1024]{2,1,0:T(8,128)}, f32[256,172]{0,1:T(8,128)}, f32[256,172]{0,1:T(8,128)}), (f32[2,32,1024]{2,1,0:T(8,128)}, f32[256,172]{0,1:T(8,128)}, f32[256,172]{0,1:T(8,128)})) %all-reduce.6.cloned.1.call-update) | async-done | bytes 614416 | tf_op jit(solution)/shard_map/psum | solution.py:124
  558.4 1.7 slice_bitcast_fusion
  560.1 1.6 copy.64
  561.7 1.6 copy.65
  (70 shorter events, 20.9 us)
Async XLA Ops:
  7.2 44.1 %copy-start = (bf16[4,16,128,128]{3,2,1,0:T(8,128)(2,1)S(1)}, bf16[4,16,128,128]{3,2,1,0:T(8,128)(2,1)}, u32[]{:S(2)}) copy-start(bf16[4,16,128,128]{3,2,1,0:T(8,128)(2,1)} %param.14) | copy-start | bytes 6291460
  22.1 15.5 %copy-start.11 = (s32[4,16]{1,0:T(4,128)S(1)}, s32[4,16]{1,0:T(4,128)}, u32[]{:S(2)}) copy-start(s32[4,16]{1,0:T(4,128)} %param.13) | copy-start | bytes 772
  22.1 15.6 %copy-start.5 = (bf16[512,32]{0,1:T(8,128)(2,1)S(1)}, bf16[512,32]{0,1:T(8,128)(2,1)}, u32[]{:S(2)}) copy-start(bf16[512,32]{0,1:T(8,128)(2,1)} %param.10) | copy-start | bytes 98308
  22.1 15.6 %copy-start.10 = (bf16[32,1024]{1,0:T(8,128)(2,1)S(1)}, bf16[32,1024]{1,0:T(8,128)(2,1)}, u32[]{:S(2)}) copy-start(bf16[32,1024]{1,0:T(8,128)(2,1)} %param.16) | copy-start | bytes 196612
  25.4 24.1 %all-to-all-start = ((bf16[64,2,1024]{2,1,0:T(2,128)(2,1)}), bf16[64,2,1024]{2,1,0:T(2,128)(2,1)S(1)}, u32[]{:S(2)}, u32[]{:S(2)}) async-start(bf16[64,2,1024]{2,1,0:T(2,128)(2,1)} %reshape.178), calls=%async_computation | async-start | bytes 524288 | tf_op jit(solution)/shard_map/all_to_all | solution.py:74
  37.5 45.1 %reduce-scatter.2.cloned.1.call-start = ((), (), s32[]{:S(2)}) async-start(), calls=%async_computation.4 | async-start | bytes 2621440 | tf_op jit(solution)/shard_map/reduce_scatter | solution.py:80
  51.3 1.6 copy-start.3
  51.3 1.6 copy-start.9
  105.2 10.9 %copy-start.7 = (bf16[256,172]{0,1:T(8,128)(2,1)S(1)}, bf16[256,172]{0,1:T(8,128)(2,1)}, u32[]{:S(2)}) copy-start(bf16[256,172]{0,1:T(8,128)(2,1)} %param.18) | copy-start | bytes 264196
  105.2 61.9 %all-to-all-start.1 = ((bf16[64,64,256]{2,1,0:T(8,128)(2,1)}), bf16[64,64,256]{2,1,0:T(8,128)(2,1)}, u32[]{:S(2)}, u32[]{:S(2)}) async-start(bf16[64,64,256]{2,1,0:T(8,128)(2,1)} %select_select_fusion), calls=%async_computation.2 | async-start | bytes 4194304 | tf_op jit(solution)/shard_map/all_to_all | solution.py:85
  116.1 105.6 %all-reduce.4.cloned.1.call-start = ((), (), s32[]{:S(2)}) async-start(), calls=%async_computation.5 | async-start | bytes 720896 | tf_op jit(solution)/shard_map/psum | solution.py:91
  174.7 3.2 copy-start.6
  174.7 48.0 %copy-start.12 = (s32[512]{0:T(512)S(1)}, s32[512]{0:T(512)}, u32[]{:S(2)}) copy-start(s32[512]{0:T(512)} %param.15) | copy-start | bytes 6148
  250.8 2.3 copy-start.2
  255.9 10.9 %copy-start.8 = (s32[1,64,64]{2,1,0:T(8,128)S(1)}, s32[1,64,64]{2,1,0:T(8,128)}, u32[]{:S(2)}) copy-start(s32[1,64,64]{2,1,0:T(8,128)} %param.11) | copy-start | bytes 49156
  255.9 11.0 %slice-start = ((f32[36,32768]{1,0:T(8,128)}), f32[4,32768]{1,0:T(4,128)S(1)}, s32[]{:S(2)}) async-start(f32[36,32768]{1,0:T(8,128)} %copy-done.2), calls=%async_computation.8 | async-start | bytes 1048576 | tf_op jit(solution)/shard_map/slice | solution.py:115
  255.9 61.9 %all-to-all-start.2 = ((bf16[64,64,256]{2,1,0:T(8,128)(2,1)}), bf16[64,64,256]{2,1,0:T(8,128)(2,1)}, u32[]{:S(2)}, u32[]{:S(2)}) async-start(bf16[64,64,256]{2,1,0:T(8,128)(2,1)} %convert_element_type.51), calls=%async_computation.3 | async-start | bytes 4194304 | tf_op jit(solution)/shard_map/all_to_all | solution.py:107
  266.7 103.8 %all-gather.2.cloned.1.call-start = ((), (), s32[]{:S(2)}) async-start(), calls=%async_computation.6 | async-start | bytes 1310720 | tf_op jit(solution)/shard_map/all_gather | solution.py:117
  321.3 23.3 %copy-start.4 = (f32[512,256]{1,0:T(8,128)S(1)}, f32[512,256]{1,0:T(8,128)}, u32[]{:S(2)}) copy-start(f32[512,256]{1,0:T(8,128)} %reduce-scatter.2.cloned.1.call-done) | copy-start | bytes 1572868
  345.7 212.8 %all-reduce.6.cloned.1.call-start = ((), (), s32[]{:S(2)}) async-start(), calls=%async_computation.7 | async-start | bytes 1245184 | tf_op jit(solution)/shard_map/psum | solution.py:124
  370.5 192.8 %copy-start.1 = (bf16[4,16,128,128]{3,2,1,0:T(8,128)(2,1)S(1)}, bf16[4,16,128,128]{3,2,1,0:T(8,128)(2,1)}, u32[]{:S(2)}) copy-start(bf16[4,16,128,128]{3,2,1,0:T(8,128)(2,1)} %param.14) | copy-start | bytes 6291460
Sparse Core Ops, SparseCore 0:
  54.8 27.8 reduce-scatter.1
  179.1 42.5 all-reduce.3
  345.8 24.6 all-gather.1
  375.2 183.2 all-reduce.5
where the time goes:
time: 572 us; the launch traced here: 571 us
  waiting for transfers between devices  259 us (45%)
  blocking collectives  129 us (23%)
  local copies, waits for them, and re-layouts  67.3 us (12%)
  other arithmetic  43.3 us (8%)
  starting transfers between devices  34 us (6%)
  matrix products  23.1 us (4%)
  between operations  15.8 us (3%)
    psum x1, blocking collectives, shards(): mean_loss = lax.psum(jnp.sum(row_loss), 'node') / node_total  129 us
    psum x1, waiting for transfers between devices, shards(): summed = lax.psum(local_grads, 'node')  54 us
    all_to_all x1, waiting for transfers between devices, shards(): lax.all_to_all(outgoing_two, 'node', split_axis=0, concat_axis=0, tiled=T...  50.7 us
    all_to_all x1, waiting for transfers between devices, shards(): lax.all_to_all(halo_back.astype(jnp.bfloat16), 'node', split_axis=0, conc...  50.3 us
    psum x1, waiting for transfers between devices, shards(): logits = lax.psum(partial_two, 'feat')  42.6 us
    gather x3, local copies, waits for them, and re-layouts, pack_rows(): picked = jnp.take(own_rows, send_rows[0].reshape(-1), axis=0)  30.2 us
    reduce_scatter x1, waiting for transfers between devices, shards(): lax.psum_scatter(partial_one, 'feat', scatter_dimension=1, tiled=True)  28 us
    scatter-add x1, other arithmetic, shards(): jax.ops.segment_sum(returned.reshape(-1, unit_count), send_rows[0].reshap...  23.3 us
  transfers between devices with their start and end apart: 7, of which 7 were waited for; matrix products, arithmetic and copies ran while one was open for 1% of the time, Pallas kernels for 0%

commit v1 on v0

--- a/solution.py
+++ b/solution.py
@@ -88,7 +88,7 @@
     agg_two = aggregate(hidden, arrived_two, tile_src, tile_val)
     partial_two = jnp.dot(hidden, w_self2, preferred_element_type=jnp.float32)
     partial_two = partial_two + jnp.dot(agg_two, w_neigh2, preferred_element_type=jnp.float32)
-    logits = lax.psum(partial_two, "feat")
+    logits = jnp.sum(lax.all_gather(partial_two, "feat"), axis=0)
     row_loss, dlogits = cross_entropy(logits, labels, grad_scale)
     mean_loss = lax.psum(jnp.sum(row_loss), "node") / node_total
     grad_pair = lax.psum(

time: 572 us -> 555 us (0.970)
  waiting for transfers between devices: 259 us -> 240 us
    psum x1 -> x0, waiting for transfers between devices: 42.6 us -> none  [shards(): logits = lax.psum(partial_two, 'feat')]
    all_gather x0 -> x1, waiting for transfers between devices: none -> 23.7 us  [shards(): logits = jnp.sum(lax.all_gather(partial_two, 'feat'), axis=0)]
where the time goes in v1:
time: 555 us; the launch traced here: 554 us
  waiting for transfers between devices  240 us (43%)
  blocking collectives  129 us (23%)
  local copies, waits for them, and re-layouts  70.4 us (13%)
  other arithmetic  42.5 us (8%)
  starting transfers between devices  34 us (6%)
  matrix products  23.1 us (4%)
  between operations  15.9 us (3%)
    psum x1, blocking collectives, shards(): mean_loss = lax.psum(jnp.sum(row_loss), 'node') / node_total  129 us
    psum x1, waiting for transfers between devices, shards(): summed = lax.psum(local_grads, 'node')  54 us
    all_to_all x1, waiting for transfers between devices, shards(): lax.all_to_all(outgoing_two, 'node', split_axis=0, concat_axis=0, tiled=T...  50.7 us
    all_to_all x1, waiting for transfers between devices, shards(): lax.all_to_all(halo_back.astype(jnp.bfloat16), 'node', split_axis=0, conc...  50.2 us
    gather x3, local copies, waits for them, and re-layouts, pack_rows(): picked = jnp.take(own_rows, send_rows[0].reshape(-1), axis=0)  30.2 us
    reduce_scatter x1, waiting for transfers between devices, shards(): lax.psum_scatter(partial_one, 'feat', scatter_dimension=1, tiled=True)  28 us
    all_gather x1, waiting for transfers between devices, shards(): logits = jnp.sum(lax.all_gather(partial_two, 'feat'), axis=0)  23.7 us
    scatter-add x1, other arithmetic, shards(): jax.ops.segment_sum(returned.reshape(-1, unit_count), send_rows[0].reshap...  23.3 us
  transfers between devices with their start and end apart: 7, of which 7 were waited for; matrix products, arithmetic and copies ran while one was open for 1% of the time, Pallas kernels for 0%

profile of v1, /device:TPU:2, one launch (start us, length us, event | category | flops | bytes accessed | tf_op | source)
XLA Modules:
  0.0 554.1 jit_solution(13253463596860846785)
XLA Ops:
  10.0 12.1 %gather_fusion = bf16[4096,32]{1,0:T(8,128)(2,1)S(1)} fusion(bf16[512,32]{1,0:T(8,128)(2,1)S(1)} %copy.35, s32[4096]{0:T(1024)S(1)} %broadcast_clamp_fusion), kind=kCustom, calls=%fused_computation | custom fusion | bytes 540672 | tf_op jit(solution)/shard_map/jit(_take)/gather | solution.py:10
  25.4 12.1 %all-to-all-start = ((bf16[64,2,1024]{2,1,0:T(2,128)(2,1)}), bf16[64,2,1024]{2,1,0:T(2,128)(2,1)S(1)}, u32[]{:S(2)}, u32[]{:S(2)}) async-start(bf16[64,2,1024]{2,1,0:T(2,128)(2,1)} %reshape.179), calls=%async_computation | async-start | bytes 524288 | tf_op jit(solution)/shard_map/all_to_all | solution.py:74
  37.7 1.8 fusion.31
  39.5 10.0 %all-to-all-done = bf16[64,2,1024]{2,1,0:T(2,128)(2,1)S(1)} async-done(((bf16[64,2,1024]{2,1,0:T(2,128)(2,1)}), bf16[64,2,1024]{2,1,0:T(2,128)(2,1)S(1)}, u32[]{:S(2)}, u32[]{:S(2)}) %all-to-all-start) | async-done | bytes 262176 | tf_op jit(solution)/shard_map/all_to_all | solution.py:74
  52.9 1.8 convolution_add_fusion
  54.7 28.0 %reduce-scatter.2.cloned.1.call-done = f32[512,256]{1,0:T(8,128)} async-done(((f32[512,1024]{1,0:T(8,128)}), f32[512,256]{1,0:T(8,128)}) %reduce-scatter.2.cloned.1.call-update) | async-done | bytes 524304 | tf_op jit(solution)/shard_map/reduce_scatter | solution.py:80
  83.9 16.9 %gather_fusion.2 = bf16[4096,256]{1,0:T(8,128)(2,1)} fusion(bf16[512,256]{1,0:T(8,128)(2,1)S(1)} %multiply_convert_fusion, s32[4096]{0:T(1024)S(1)} %broadcast_clamp_fusion), kind=kCustom, calls=%fused_computation.2 | custom fusion | bytes 4210688 | tf_op jit(solution)/shard_map/jit(_take)/gather | solution.py:10
  100.8 4.4 select_select_fusion
  105.2 10.9 %all-to-all-start.1 = ((bf16[64,64,256]{2,1,0:T(8,128)(2,1)}), bf16[64,64,256]{2,1,0:T(8,128)(2,1)}, u32[]{:S(2)}, u32[]{:S(2)}) async-start(bf16[64,64,256]{2,1,0:T(8,128)(2,1)} %select_select_fusion), calls=%async_computation.2 | async-start | bytes 4194304 | tf_op jit(solution)/shard_map/all_to_all | solution.py:85
  116.4 50.7 %all-to-all-done.1 = bf16[64,64,256]{2,1,0:T(8,128)(2,1)} async-done(((bf16[64,64,256]{2,1,0:T(8,128)(2,1)}), bf16[64,64,256]{2,1,0:T(8,128)(2,1)}, u32[]{:S(2)}, u32[]{:S(2)}) %all-to-all-start.1) | async-done | bytes 2097184 | tf_op jit(solution)/shard_map/all_to_all | solution.py:85
  167.1 3.2 pad_maximum_fusion
  170.3 4.4 gather_fusion.3
  174.7 3.2 fusion.7
  179.0 23.7 %all-gather.6.cloned.1.call-done = f32[2048,172]{0,1:T(8,128)} async-done(((f32[512,172]{0,1:T(8,128)}), f32[2048,172]{0,1:T(8,128)}) %all-gather.6.cloned.1.call-update) | async-done | bytes 1409040 | tf_op jit(solution)/shard_map/all_gather | solution.py:91
  202.7 3.0 reshape.170
  205.8 2.2 reduce_sum.36
  208.5 4.5 convolution_bitcast_fusion
  213.0 8.7 %copy.41 = f32[4,16,128,256]{3,2,1,0:T(8,128)} copy(f32[4,16,128,256]{2,3,1,0:T(8,128)} %convolution_bitcast_fusion) | data formatting | bytes 16777216 | tf_op jit(solution)/shard_map/bkij,bih->bkjh/dot_general | solution.py:26
  221.7 8.1 %copy.49 = f32[8,8,128,256]{3,1,2,0:T(8,128)S(1)} copy(f32[8,8,128,256]{3,2,1,0:T(8,128)} %bitcast.92) | data formatting | bytes 16777216
  229.8 4.3 fusion.26
  234.2 2.3 copy-done.2
  236.8 2.4 convert_element_type.51
  239.2 10.9 %all-to-all-start.2 = ((bf16[64,64,256]{2,1,0:T(8,128)(2,1)}), bf16[64,64,256]{2,1,0:T(8,128)(2,1)}, u32[]{:S(2)}, u32[]{:S(2)}) async-start(bf16[64,64,256]{2,1,0:T(8,128)(2,1)} %convert_element_type.51), calls=%async_computation.3 | async-start | bytes 4194304 | tf_op jit(solution)/shard_map/all_to_all | solution.py:107
  250.9 50.2 %all-to-all-done.2 = bf16[64,64,256]{2,1,0:T(8,128)(2,1)} async-done(((bf16[64,64,256]{2,1,0:T(8,128)(2,1)}), bf16[64,64,256]{2,1,0:T(8,128)(2,1)}, u32[]{:S(2)}, u32[]{:S(2)}) %all-to-all-start.2) | async-done | bytes 2097184 | tf_op jit(solution)/shard_map/all_to_all | solution.py:107
  301.1 3.5 convert_select_fusion
  304.6 23.3 %scatter_fusion = f32[512,256]{1,0:T(8,128)S(1)} fusion(f32[512,256]{1,0:T(8,128)S(1)} %convolution_add_fusion.1, s32[4096]{0:T(1024)S(1)} %reshape.164, f32[4096,256]{1,0:T(8,128)} %bitcast.94), kind=kCustom, calls=%fused_computation.4 | custom fusion | flops 1048576 | bytes 12599296 | tf_op jit(solution)/shard_map/scatter-add | solution.py:112
  330.9 22.8 %all-gather.4.cloned.1.call-done = bf16[512,1024]{1,0:T(8,128)(2,1)} async-done(((bf16[512,256]{1,0:T(8,128)(2,1)}), bf16[512,1024]{1,0:T(8,128)(2,1)}) %all-gather.4.cloned.1.call-update) | async-done | bytes 1048592 | tf_op jit(solution)/shard_map/all_gather | solution.py:117
  353.6 1.7 convolution_bitcast_fusion.2
  358.2 128.7 %psum.28 = f32[]{:T(128)} all-reduce(f32[]{:T(128)} %subtract_reduce_fusion), channel_id=1, replica_groups=mesh['node'=64,'feat'=4] {'node'}, use_global_device_ids=true, to_apply=%region_6.7 | all-reduce | flops 1 | bytes 8 | tf_op jit(solution)/shard_map/psum | solution.py:93
  487.6 54.0 %all-reduce.3.cloned.1.call-done = (f32[2,32,1024]{2,1,0:T(8,128)}, f32[256,172]{0,1:T(8,128)}, f32[256,172]{0,1:T(8,128)}) async-done(((f32[2,32,1024]{2,1,0:T(8,128)}, f32[256,172]{0,1:T(8,128)}, f32[256,172]{0,1:T(8,128)}), (f32[2,32,1024]{2,1,0:T(8,128)}, f32[256,172]{0,1:T(8,128)}, f32[256,172]{0,1:T(8,128)})) %all-reduce.3.cloned.1.call-update) | async-done | bytes 614416 | tf_op jit(solution)/shard_map/psum | solution.py:124
  541.6 1.7 slice_bitcast_fusion
  544.9 1.6 copy.64
  (72 shorter events, 21.1 us)
Async XLA Ops:
  7.2 44.1 %copy-start = (bf16[4,16,128,128]{3,2,1,0:T(8,128)(2,1)S(1)}, bf16[4,16,128,128]{3,2,1,0:T(8,128)(2,1)}, u32[]{:S(2)}) copy-start(bf16[4,16,128,128]{3,2,1,0:T(8,128)(2,1)} %param.14) | copy-start | bytes 6291460
  22.1 15.5 %copy-start.11 = (s32[4,16]{1,0:T(4,128)S(1)}, s32[4,16]{1,0:T(4,128)}, u32[]{:S(2)}) copy-start(s32[4,16]{1,0:T(4,128)} %param.13) | copy-start | bytes 772
  22.1 15.6 %copy-start.5 = (bf16[512,32]{0,1:T(8,128)(2,1)S(1)}, bf16[512,32]{0,1:T(8,128)(2,1)}, u32[]{:S(2)}) copy-start(bf16[512,32]{0,1:T(8,128)(2,1)} %param.10) | copy-start | bytes 98308
  22.1 15.6 %copy-start.10 = (bf16[32,1024]{1,0:T(8,128)(2,1)S(1)}, bf16[32,1024]{1,0:T(8,128)(2,1)}, u32[]{:S(2)}) copy-start(bf16[32,1024]{1,0:T(8,128)(2,1)} %param.16) | copy-start | bytes 196612
  25.4 24.1 %all-to-all-start = ((bf16[64,2,1024]{2,1,0:T(2,128)(2,1)}), bf16[64,2,1024]{2,1,0:T(2,128)(2,1)S(1)}, u32[]{:S(2)}, u32[]{:S(2)}) async-start(bf16[64,2,1024]{2,1,0:T(2,128)(2,1)} %reshape.179), calls=%async_computation | async-start | bytes 524288 | tf_op jit(solution)/shard_map/all_to_all | solution.py:74
  37.5 45.1 %reduce-scatter.2.cloned.1.call-start = ((), (), s32[]{:S(2)}) async-start(), calls=%async_computation.4 | async-start | bytes 2621440 | tf_op jit(solution)/shard_map/reduce_scatter | solution.py:80
  51.3 1.6 copy-start.3
  51.3 1.6 copy-start.9
  105.2 10.9 %copy-start.7 = (bf16[256,172]{0,1:T(8,128)(2,1)S(1)}, bf16[256,172]{0,1:T(8,128)(2,1)}, u32[]{:S(2)}) copy-start(bf16[256,172]{0,1:T(8,128)(2,1)} %param.18) | copy-start | bytes 264196
  105.2 61.9 %all-to-all-start.1 = ((bf16[64,64,256]{2,1,0:T(8,128)(2,1)}), bf16[64,64,256]{2,1,0:T(8,128)(2,1)}, u32[]{:S(2)}, u32[]{:S(2)}) async-start(bf16[64,64,256]{2,1,0:T(8,128)(2,1)} %select_select_fusion), calls=%async_computation.2 | async-start | bytes 4194304 | tf_op jit(solution)/shard_map/all_to_all | solution.py:85
  116.1 86.7 %all-gather.6.cloned.1.call-start = ((), (), s32[]{:S(2)}) async-start(), calls=%async_computation.6 | async-start | bytes 1802240 | tf_op jit(solution)/shard_map/all_gather | solution.py:91
  174.7 3.2 copy-start.6
  179.0 29.0 %copy-start.12 = (s32[512]{0:T(512)S(1)}, s32[512]{0:T(512)}, u32[]{:S(2)}) copy-start(s32[512]{0:T(512)} %param.15) | copy-start | bytes 6148
  234.1 2.3 copy-start.2
  239.2 10.9 %copy-start.8 = (s32[1,64,64]{2,1,0:T(8,128)S(1)}, s32[1,64,64]{2,1,0:T(8,128)}, u32[]{:S(2)}) copy-start(s32[1,64,64]{2,1,0:T(8,128)} %param.11) | copy-start | bytes 49156
  239.2 11.0 %slice-start = ((f32[36,32768]{1,0:T(8,128)}), f32[4,32768]{1,0:T(4,128)S(1)}, s32[]{:S(2)}) async-start(f32[36,32768]{1,0:T(8,128)} %copy-done.2), calls=%async_computation.8 | async-start | bytes 1048576 | tf_op jit(solution)/shard_map/slice | solution.py:115
  239.2 61.9 %all-to-all-start.2 = ((bf16[64,64,256]{2,1,0:T(8,128)(2,1)}), bf16[64,64,256]{2,1,0:T(8,128)(2,1)}, u32[]{:S(2)}, u32[]{:S(2)}) async-start(bf16[64,64,256]{2,1,0:T(8,128)(2,1)} %convert_element_type.51), calls=%async_computation.3 | async-start | bytes 4194304 | tf_op jit(solution)/shard_map/all_to_all | solution.py:107
  250.1 103.5 %all-gather.4.cloned.1.call-start = ((), (), s32[]{:S(2)}) async-start(), calls=%async_computation.5 | async-start | bytes 1310720 | tf_op jit(solution)/shard_map/all_gather | solution.py:117
  304.6 23.3 %copy-start.4 = (f32[512,256]{1,0:T(8,128)S(1)}, f32[512,256]{1,0:T(8,128)}, u32[]{:S(2)}) copy-start(f32[512,256]{1,0:T(8,128)} %reduce-scatter.2.cloned.1.call-done) | copy-start | bytes 1572868
  329.0 212.5 %all-reduce.3.cloned.1.call-start = ((), (), s32[]{:S(2)}) async-start(), calls=%async_computation.7 | async-start | bytes 1245184 | tf_op jit(solution)/shard_map/psum | solution.py:124
  353.6 192.8 %copy-start.1 = (bf16[4,16,128,128]{3,2,1,0:T(8,128)(2,1)S(1)}, bf16[4,16,128,128]{3,2,1,0:T(8,128)(2,1)}, u32[]{:S(2)}) copy-start(bf16[4,16,128,128]{3,2,1,0:T(8,128)(2,1)} %param.14) | copy-start | bytes 6291460
Sparse Core Ops, SparseCore 0:
  54.8 27.8 reduce-scatter.1
  179.1 23.6 all-gather.5
  329.2 24.4 all-gather.3
  358.3 183.2 all-reduce.2
